TPU v7x, 32 devices: a whole 2x2x4 slice. The times are simulated.
32 devices in a mesh: row: 8 (over y, x, core), col: 4 (over z).
Axes of the slice: x: 2, y: 2, z: 4, core: 2. Of those that a mesh axis runs over, the one named last changes fastest.
Arguments:
- coeffs: bfloat16 [6144, 4096], P('row', 'col'), may hold values from -0.00390625 to 0.00390625
- occupation: float32 [4096], P('col'), may hold values from 0.5 to 2
- basis_on_grid: bfloat16 [320, 512, 512], P('row'), may hold values from -6 to 6
- basis_map: int32 [320, 512], P('row'), may hold values from 0 to 6143, as said below
- basis_count: int32 [320], P('row'), may hold values from 256 to 512
- batch_atom: int32 [320], P('row'), may hold values from 0 to 63
- harmonics: float32 [320, 49, 512], P('row'), may hold values from -0.25 to 0.25
Outputs:
- density: float32 [320, 512], P('row', 'col')
- moments: float32 [64, 49], replicated
Inputs may be any that keep to these rules, and one draw needn't show every extreme that they name: `basis_map`: the slots of one batch name distinct basis functions. With R = 768 and o = b // 40, batch b names only basis functions q * R + (o * 96 + w) mod R with 0 <= q < 8 and 0 <= w < 96.
All inputs are finite; a program needn't handle non-finite values.
Results may differ from a plain program's by a relative error of at most 0.0003.
Values may be sent and summed in bfloat16 or wider, within the bound.
No kernel may reach another device: no remote copies, remote signals or barrier semaphores. Data moves between devices by JAX's collectives and lax.ppermute only.
A program may use at most 192 MiB of HBM per device.

v0:
```python
import jax
import jax.numpy as jnp
from jax import lax
from jax.sharding import PartitionSpec as P

WIN = 96
NATOM = 64


def shards(coeffs, occupation, basis_on_grid, basis_map, basis_count, batch_atom, harmonics):
    batches, points, slots = basis_on_grid.shape
    owned = coeffs.shape[0]
    owners = lax.axis_size("row")
    target = lax.broadcasted_iota(jnp.int32, (owners, WIN), 0)
    offset = lax.broadcasted_iota(jnp.int32, (owners, WIN), 1)
    outgoing_ids = jnp.mod(target * WIN + offset, owned).reshape(-1)
    outgoing = jnp.take(coeffs, outgoing_ids, axis=0)
    window = lax.all_to_all(outgoing, "row", split_axis=0, concat_axis=0, tiled=True)
    start = jnp.mod(lax.axis_index("row") * WIN, owned)
    source = basis_map // owned
    within = jnp.mod(basis_map % owned - start, owned)
    local_ids = source * WIN + within
    selected = jnp.take(window, local_ids, axis=0)
    slot_ids = lax.broadcasted_iota(jnp.int32, (batches, slots), 1)
    keep = slot_ids < basis_count[:, None]
    masked = jnp.where(keep[:, None, :], basis_on_grid, jnp.zeros_like(basis_on_grid))
    orbital = jnp.einsum("bps,bsk->bpk", masked, selected, preferred_element_type=jnp.float32)
    partial_density = jnp.sum(orbital * orbital * occupation[None, None, :], axis=2)
    atom_ids = lax.broadcasted_iota(jnp.int32, (batches, NATOM), 1)
    member = (batch_atom[:, None] == atom_ids).astype(jnp.float32)
    full_density = lax.psum(partial_density, "col")
    local_moment = jnp.einsum(
        "blp,bp->bl", harmonics, full_density, precision=lax.Precision.HIGHEST
    )
    atom_part = jnp.dot(member.T, local_moment, precision=lax.Precision.HIGHEST)
    moments = lax.psum(atom_part, "row")
    share = points // lax.axis_size("col")
    density = lax.dynamic_slice_in_dim(full_density, lax.axis_index("col") * share, share, 1)
    return (density, moments)


def solution(mesh):
    placed = (
        P("row", "col"),
        P("col"),
        P("row", None, None),
        P("row", None),
        P("row"),
        P("row"),
        P("row", None, None),
    )
    return jax.shard_map(
        shards, mesh=mesh, in_specs=placed, out_specs=(P("row", "col"), P()), check_vma=False
    )
```

profile of v0, /device:TPU:0, one launch (start us, length us, event | category | flops | bytes accessed | tf_op | source)
XLA Modules:
  0.0 228.4 jit_solution(9429908495071229577)
XLA Ops:
  7.2 0.0 copy-start
  7.2 0.1 add_remainder_fusion
  7.3 0.1 compare_and_fusion.1
  7.4 0.1 rem.52
  7.5 1.1 copy-done
  8.6 2.8 %gather_fusion = bf16[768,1024]{1,0:T(8,128)(2,1)S(1)} fusion(bf16[768,1024]{1,0:T(8,128)(2,1)S(1)} %copy-done, s32[1024]{0:T(1024)S(1)} %pad_clamp_fusion), kind=kCustom, calls=%fused_computation | custom fusion | bytes 3148800 | tf_op jit(solution)/shard_map/jit(_take)/gather | solution.py:17
  11.4 1.4 broadcast_select_fusion
  12.8 5.2 %all-to-all-start = ((bf16[8,96,1024]{2,1,0:T(8,128)(2,1)}), bf16[8,96,1024]{2,1,0:T(8,128)(2,1)S(1)}, u32[]{:S(2)}, u32[]{:S(2)}) async-start(bf16[8,96,1024]{2,1,0:T(8,128)(2,1)} %broadcast_select_fusion), calls=%async_computation | async-start | bytes 3145728 | tf_op jit(solution)/shard_map/all_to_all | solution.py:18
  18.0 0.0 all-reduce.2.cloned.1.call-start
  18.0 1.0 compare_and_fusion
  19.1 0.7 iota_compare_fusion
  19.9 19.1 %all-to-all-done = bf16[8,96,1024]{2,1,0:T(8,128)(2,1)S(1)} async-done(((bf16[8,96,1024]{2,1,0:T(8,128)(2,1)}), bf16[8,96,1024]{2,1,0:T(8,128)(2,1)S(1)}, u32[]{:S(2)}, u32[]{:S(2)}) %all-to-all-start) | async-done | bytes 1572896 | tf_op jit(solution)/shard_map/all_to_all | solution.py:18
  39.0 0.0 copy-start.2
  39.0 87.0 %gather_fusion.1 = bf16[20480,1024]{1,0:T(8,128)(2,1)} fusion(bf16[768,1024]{1,0:T(8,128)(2,1)S(1)} %bitcast.9, s32[20480]{0:T(1024)S(1)} %broadcast_clamp_fusion), kind=kCustom, calls=%fused_computation.1 | custom fusion | bytes 83968000 | tf_op jit(solution)/shard_map/jit(_take)/gather | solution.py:23
  125.9 0.0 copy-done.2
  125.9 0.0 copy-start.3
  125.9 0.0 copy-start.1
  125.9 29.3 %multiply_reduce_fusion = f32[40,512]{1,0:T(8,128)} fusion(f32[1024]{0:T(1024)S(1)} %copy-done.2, bf16[40,512,1024]{2,1,0:T(8,128)(2,1)} %bitcast.10, pred[40,512]{1,0:T(8,128)(4,1)S(1)} %get-tuple-element.2, bf16[40,512,512]{2,1,0:T(8,128)(2,1)} %param.9, pred[40,512]{1,0:T(8,128)(4,1)S(1)} %iota_compare_fusion), kind=kOutput, calls=%fused_computation.2 | convolution fusion | flops 21569187840 | bytes 63041536 | tf_op jit(solution)/shard_map/bps,bsk->bpk/dot_general | solution.py:27
  155.2 0.0 all-reduce.2.cloned.1.call-update
  155.3 33.8 %all-reduce.2.cloned.1.call-done = f32[40,512]{1,0:T(8,128)} async-done(((f32[40,512]{1,0:T(8,128)}), f32[40,512]{1,0:T(8,128)}) %all-reduce.2.cloned.1.call-update) | async-done | bytes 81936 | tf_op jit(solution)/shard_map/psum | solution.py:31
  189.0 7.9 %fusion.11 = f32[40,1,49]{2,1,0:T(1,128)S(1)} fusion(f32[40,49,512]{2,0,1:T(8,128)} %param.13, f32[40,512,1]{1,0,2:T(8,128)} %bitcast.14), kind=kOutput, calls=%fused_computation.10 | convolution fusion | flops 12042240 | bytes 4103840 | tf_op jit(solution)/shard_map/blp,bp->bl/dot_general | solution.py:32
  196.9 0.0 copy-done.3
  196.9 0.2 fusion.19
  197.2 23.0 %psum.15 = f32[64,49]{0,1:T(8,128)} all-reduce(f32[64,49]{0,1:T(8,128)S(1)} %fusion.19), channel_id=1, replica_groups=mesh['row'=8,'col'=4] {'row'}, use_global_device_ids=true, to_apply=%region_2.3 | all-reduce | flops 3136 | bytes 25088 | tf_op jit(solution)/shard_map/psum | solution.py:36
  220.2 1.3 constant_dynamic-slice_fusion
  221.5 0.0 copy-done.1
  (5 shorter events, 0.1 us)
Async XLA Ops:
  7.2 1.4 copy-start
  12.8 26.2 %all-to-all-start = ((bf16[8,96,1024]{2,1,0:T(8,128)(2,1)}), bf16[8,96,1024]{2,1,0:T(8,128)(2,1)S(1)}, u32[]{:S(2)}, u32[]{:S(2)}) async-start(bf16[8,96,1024]{2,1,0:T(8,128)(2,1)} %broadcast_select_fusion), calls=%async_computation | async-start | bytes 3145728 | tf_op jit(solution)/shard_map/all_to_all | solution.py:18
  18.0 171.1 %all-reduce.2.cloned.1.call-start = ((), (), s32[]{:S(2)}) async-start(), calls=%async_computation.1 | async-start | bytes 163840 | tf_op jit(solution)/shard_map/psum | solution.py:31
  39.0 87.0 %copy-start.2 = (f32[1024]{0:T(1024)S(1)}, f32[1024]{0:T(1024)}, u32[]{:S(2)}) copy-start(f32[1024]{0:T(1024)} %param.8) | copy-start | bytes 12292
  125.9 71.0 %copy-start.3 = (s32[40]{0:T(128)S(1)}, s32[40]{0:T(128)}, u32[]{:S(2)}) copy-start(s32[40]{0:T(128)} %param.12) | copy-start | bytes 484
  125.9 95.6 %copy-start.1 = (bf16[768,1024]{1,0:T(8,128)(2,1)S(1)}, bf16[768,1024]{1,0:T(8,128)(2,1)}, u32[]{:S(2)}) copy-start(bf16[768,1024]{1,0:T(8,128)(2,1)} %param.7) | copy-start | bytes 4718596
Sparse Core Ops, SparseCore 0:
  155.4 33.6 all-reduce.1
where the time goes:
time: 229 us; the launch traced here: 228 us
  local copies, waits for them, and re-layouts  92.3 us (40%)
  waiting for transfers between devices  52.9 us (23%)
  matrix products  37.5 us (16%)
  blocking collectives  23 us (10%)
  between operations  14.1 us (6%)
  starting transfers between devices  5.24 us (2%)
  other arithmetic  3.37 us (1%)
    gather x1, local copies, waits for them, and re-layouts, shards(): selected = jnp.take(window, local_ids, axis=0)  87 us
    psum x1, waiting for transfers between devices, shards(): full_density = lax.psum(partial_density, 'col')  33.8 us
    dot_general x1, matrix products, shards(): jnp.einsum('bps,bsk->bpk', masked, selected, preferred_element_type=jnp.f...  29.3 us
    psum x1, blocking collectives, shards(): moments = lax.psum(atom_part, 'row')  23 us
    all_to_all x1, waiting for transfers between devices, shards(): lax.all_to_all(outgoing, 'row', split_axis=0, concat_axis=0, tiled=True)  19.1 us
    dot_general x1, matrix products, shards(): jnp.einsum('blp,bp->bl', harmonics, full_density, precision=lax.Precision...  7.89 us
    all_to_all x1, starting transfers between devices, shards(): lax.all_to_all(outgoing, 'row', split_axis=0, concat_axis=0, tiled=True)  5.2 us
  transfers between devices with their start and end apart: 2, of which 2 were waited for; matrix products, arithmetic and copies ran while one was open for 1% of the time, Pallas kernels for 0%

commit v1 on v0

v1 whole, which is shorter than its diff:
```python
import jax
import jax.numpy as jnp
from jax import lax
from jax.experimental import pallas as pl
from jax.experimental.pallas import tpu as pltpu
from jax.sharding import PartitionSpec as P

WIN = 96
NATOM = 64


def spread_kernel(ids_ref, values_ref, out_ref):
    wide = out_ref.shape[1]
    slots = ids_ref.shape[2]
    rows = lax.broadcasted_iota(jnp.int32, (wide, slots), 0)
    place = jnp.where(rows == ids_ref[0], 1.0, 0.0).astype(jnp.bfloat16)
    out = lax.dot_general(
        place, values_ref[0], (((1,), (1,)), ((), ())), preferred_element_type=jnp.float32
    )
    out_ref[0] = out.astype(jnp.bfloat16)


def spread(ids, values, wide):
    batches, points, slots = values.shape
    return pl.pallas_call(
        spread_kernel,
        grid=(batches,),
        in_specs=[
            pl.BlockSpec((1, 1, slots), lambda b: (b, 0, 0)),
            pl.BlockSpec((1, points, slots), lambda b: (b, 0, 0)),
        ],
        out_specs=pl.BlockSpec((1, wide, points), lambda b: (b, 0, 0)),
        out_shape=jax.ShapeDtypeStruct((batches, wide, points), jnp.bfloat16),
        compiler_params=pltpu.CompilerParams(dimension_semantics=("arbitrary",)),
        cost_estimate=pl.CostEstimate(
            flops=2 * batches * points * slots * wide,
            bytes_accessed=2 * batches * points * (slots + wide),
            transcendentals=0,
        ),
    )(ids[:, None, :], values)


def density_kernel(atom_ref, spread_ref, window_ref, occ_ref, harm_ref, den_ref, mom_ref, turned):
    b = pl.program_id(0)

    @pl.when(b == 0)
    def _():
        turned[...] = window_ref[...].T
        mom_ref[...] = jnp.zeros_like(mom_ref)

    states, _ = turned.shape
    points = spread_ref.shape[2]
    step = min(256, states)
    values = spread_ref[0]
    total = jnp.zeros((8, points), jnp.float32)
    for first in range(0, states, step):
        orbital = jnp.dot(turned[first:first + step, :], values, preferred_element_type=jnp.float32)
        weight = jnp.tile(occ_ref[first:first + step, :], (1, points // occ_ref.shape[1]))
        scaled = orbital * orbital * weight
        total = total + jnp.sum(scaled.reshape(step // 8, 8, points), axis=0)
    density = jnp.sum(total, axis=0, keepdims=True)
    den_ref[0] = density
    local = jnp.sum(harm_ref[0] * density, axis=1, keepdims=True)
    atoms = lax.broadcasted_iota(jnp.int32, mom_ref.shape, 1)
    mom_ref[...] += jnp.where(atoms == atom_ref[b], local, 0.0)


def densities(batch_atom, spreads, window, occupation, harmonics):
    batches, wide, points = spreads.shape
    states = window.shape[1]
    parts = harmonics.shape[1]
    lanes = min(128, points)
    occ = jnp.broadcast_to(occupation[:, None], (states, lanes))
    return pl.pallas_call(
        density_kernel,
        grid_spec=pltpu.PrefetchScalarGridSpec(
            num_scalar_prefetch=1,
            grid=(batches,),
            in_specs=[
                pl.BlockSpec((1, wide, points), lambda b, a: (b, 0, 0)),
                pl.BlockSpec((wide, states), lambda b, a: (0, 0)),
                pl.BlockSpec((states, lanes), lambda b, a: (0, 0)),
                pl.BlockSpec((1, parts, points), lambda b, a: (b, 0, 0)),
            ],
            out_specs=[
                pl.BlockSpec((1, 1, points), lambda b, a: (b, 0, 0)),
                pl.BlockSpec((parts, NATOM), lambda b, a: (0, 0)),
            ],
            scratch_shapes=[pltpu.VMEM((states, wide), jnp.bfloat16)],
        ),
        out_shape=[
            jax.ShapeDtypeStruct((batches, 1, points), jnp.float32),
            jax.ShapeDtypeStruct((parts, NATOM), jnp.float32),
        ],
        compiler_params=pltpu.CompilerParams(dimension_semantics=("arbitrary",)),
        cost_estimate=pl.CostEstimate(
            flops=2 * batches * points * wide * states,
            bytes_accessed=2 * batches * points * wide,
            transcendentals=0,
        ),
    )(batch_atom, spreads, window, occ, harmonics)


def shards(coeffs, occupation, basis_on_grid, basis_map, basis_count, batch_atom, harmonics):
    batches, points, slots = basis_on_grid.shape
    owned = coeffs.shape[0]
    owners = lax.axis_size("row")
    wide = owners * WIN
    if wide == owned:
        outgoing = coeffs
    else:
        target = lax.broadcasted_iota(jnp.int32, (owners, WIN), 0)
        offset = lax.broadcasted_iota(jnp.int32, (owners, WIN), 1)
        outgoing = jnp.take(coeffs, jnp.mod(target * WIN + offset, owned).reshape(-1), axis=0)
    window = lax.all_to_all(outgoing, "row", split_axis=0, concat_axis=0, tiled=True)
    start = jnp.mod(lax.axis_index("row") * WIN, owned)
    source = basis_map // owned
    within = jnp.mod(basis_map % owned - start, owned)
    local_ids = source * WIN + within
    slot_ids = lax.broadcasted_iota(jnp.int32, (batches, slots), 1)
    local_ids = jnp.where(slot_ids < basis_count[:, None], local_ids, -1)
    spreads = spread(local_ids, basis_on_grid, wide)
    partial, atom_part = densities(batch_atom, spreads, window, occupation, harmonics)
    density = lax.psum_scatter(partial[:, 0, :], "col", scatter_dimension=1, tiled=True)
    moments = lax.psum(atom_part, ("row", "col")).T
    return (density, moments)


def solution(mesh):
    placed = (
        P("row", "col"),
        P("col"),
        P("row", None, None),
        P("row", None),
        P("row"),
        P("row"),
        P("row", None, None),
    )
    return jax.shard_map(
        shards, mesh=mesh, in_specs=placed, out_specs=(P("row", "col"), P()), check_vma=False
    )
```

time: 229 us -> 163 us (0.71)
  Pallas kernels: 0 us -> 88.8 us
  local copies, waits for them, and re-layouts: 92.3 us -> 10.1 us
  waiting for transfers between devices: 52.9 us -> 0.02 us
  matrix products: 37.5 us -> 0 us
  blocking collectives: 23 us -> 41.8 us
  other arithmetic: 3.37 us -> 1.03 us
    gather x2 -> x0, local copies, waits for them, and re-layouts: 89.8 us -> none  [the longest x1 87 us: shards(): selected = jnp.take(window, local_ids, axis=0)]
    pallas_call x0 -> x2, Pallas kernels: none -> 88.8 us  [the longest x1 48.1 us: densities(): pl.pallas_call(density_kernel, grid_spec=pltpu.PrefetchScalarGridSpec(num...]
    dot_general x3 -> x0, matrix products: 37.5 us -> none  [the longest x1 29.3 us: shards(): jnp.einsum('bps,bsk->bpk', masked, selected, preferred_element_type=jnp.f...]
    psum x1 -> x0, waiting for transfers between devices: 33.8 us -> none  [shards(): full_density = lax.psum(partial_density, 'col')]
    all_to_all x1, waiting for transfers between devices: 19.1 us -> 0.01 us  [shards(): lax.all_to_all(outgoing, 'row', split_axis=0, concat_axis=0, tiled=True)]
    psum x1, blocking collectives: 23 us -> 41.8 us  [shards(): moments = lax.psum(atom_part, ('row', 'col')).T]
    unnamed x9 -> x6, local copies, waits for them, and re-layouts: 1.15 us -> 8.24 us
  transfers between devices with their start and end apart: 2 -> 2, of which waited for: 2 -> 0; matrix products, arithmetic and copies ran while one was open for 1% -> 5% of each run, Pallas kernels for 0% -> 25%
where the time goes in v1:
time: 163 us; the launch traced here: 161 us
  Pallas kernels  88.8 us (54%)
  blocking collectives  41.8 us (26%)
  between operations  14.1 us (9%)
  local copies, waits for them, and re-layouts  10.1 us (6%)
  starting transfers between devices  5.25 us (3%)
    pallas_call x1, Pallas kernels, densities(): pl.pallas_call(density_kernel, grid_spec=pltpu.PrefetchScalarGridSpec(num...  48.1 us
    psum x1, blocking collectives, shards(): moments = lax.psum(atom_part, ('row', 'col')).T  41.8 us
    pallas_call x1, Pallas kernels, spread(): pl.pallas_call(spread_kernel, grid=(batches,), in_specs=[pl.BlockSpec((1,...  40.8 us
    unnamed x6, local copies, waits for them, and re-layouts  8.24 us
    all_to_all x1, starting transfers between devices, shards(): lax.all_to_all(outgoing, 'row', split_axis=0, concat_axis=0, tiled=True)  5.21 us
  transfers between devices with their start and end apart: 2, of which 0 were waited for; matrix products, arithmetic and copies ran while one was open for 5% of the time, Pallas kernels for 25%

profile of v1, /device:TPU:0, one launch (start us, length us, event | category | flops | bytes accessed | tf_op | source)
XLA Modules:
  0.0 161.1 jit_solution(17629079902791837523)
XLA Ops:
  7.2 5.2 %all-to-all-start = ((bf16[8,96,1024]{2,1,0:T(8,128)(2,1)}), bf16[8,96,1024]{2,1,0:T(8,128)(2,1)S(1)}, u32[]{:S(2)}, u32[]{:S(2)}) async-start(bf16[8,96,1024]{2,1,0:T(8,128)(2,1)} %bitcast.6), calls=%async_computation | async-start | bytes 3145728 | tf_op jit(solution)/shard_map/all_to_all | solution.py:115
  12.4 0.0 reduce-scatter.2.cloned.1.call-start
  12.4 1.0 fusion.2
  13.5 0.7 broadcast_in_dim.6.ids_ref
  14.2 6.5 %copy.9.harm_ref = f32[40,49,512]{2,1,0:T(8,128)} copy(f32[40,49,512]{2,0,1:T(8,128)} %param.13) | data formatting | bytes 8028160 | tf_op args[6]
  20.7 0.0 copy-start.1
  20.7 40.8 %shard_map.86.spread_ref = bf16[40,768,512]{2,1,0:T(8,128)(2,1)} custom-call(s32[40,1,512]{2,1,0:T(1,128)} %broadcast_in_dim.6.ids_ref, bf16[40,512,512]{2,1,0:T(8,128)(2,1)} %values_ref.1), custom_call_target="tpu_custom_call" | custom-call | flops 16106127360 | bytes 52428800 | tf_op jit(solution)/shard_map/pallas_call | solution.py:25
  61.5 0.0 all-to-all-done
  61.5 0.0 copy-start
  61.5 0.0 copy-done.1
  61.5 1.2 broadcast_in_dim.7.occ_ref
  62.7 0.2 copy-done
  62.8 48.1 %shard_map.87 = (f32[40,1,512]{2,1,0:T(1,128)}, f32[49,64]{1,0:T(8,128)}) custom-call(s32[40]{0:T(128)} %atom_ref.1, bf16[40,768,512]{2,1,0:T(8,128)(2,1)} %shard_map.86.spread_ref, bf16[768,1024]{1,0:T(8,128)(2,1)} %bitcast.7, f32[1024,128]{1,0:T(8,128)} %broadcast_in_dim.7.occ_ref, f32[40,49,512]{2,1,0:T(8,128)} %copy.9.harm_ref), custom_call_target="tpu_custom_call" | custom-call | flops 32212254720 | bytes 31457280 | tf_op jit(solution)/shard_map/pallas_call | solution.py:74
  110.9 1.5 copy.12
  112.4 0.0 reduce-scatter.2.cloned.1.call-update
  112.4 41.8 %psum.7 = f32[64,49]{0,1:T(8,128)} all-reduce(f32[64,49]{0,1:T(8,128)} %bitcast.9), channel_id=1, replica_groups=mesh['row'=8,'col'=4] {'row','col'}, use_global_device_ids=true, to_apply=%region_1.2 | all-reduce | flops 3136 | bytes 25088 | tf_op jit(solution)/shard_map/psum | solution.py:125
  154.2 0.0 reduce-scatter.2.cloned.1.call-done
Async XLA Ops:
  7.2 54.3 %all-to-all-start = ((bf16[8,96,1024]{2,1,0:T(8,128)(2,1)}), bf16[8,96,1024]{2,1,0:T(8,128)(2,1)S(1)}, u32[]{:S(2)}, u32[]{:S(2)}) async-start(bf16[8,96,1024]{2,1,0:T(8,128)(2,1)} %bitcast.6), calls=%async_computation | async-start | bytes 3145728 | tf_op jit(solution)/shard_map/all_to_all | solution.py:115
  12.4 141.9 %reduce-scatter.2.cloned.1.call-start = ((), (), s32[]{:S(2)}) async-start(), calls=%async_computation.2 | async-start | bytes 102400 | tf_op jit(solution)/shard_map/reduce_scatter | solution.py:124
  20.7 40.8 %copy-start.1 = (f32[1024]{0:T(1024)S(1)}, f32[1024]{0:T(1024)}, u32[]{:S(2)}) copy-start(f32[1024]{0:T(1024)} %param.8) | copy-start | bytes 12292
  61.5 1.4 copy-start
Sparse Core Ops, SparseCore 0:
  112.6 21.0 reduce-scatter.1

commit v2 on v1

v2 whole, which is shorter than its diff:
```python
import jax
import jax.numpy as jnp
from jax import lax
from jax.experimental import pallas as pl
from jax.experimental.pallas import tpu as pltpu
from jax.sharding import PartitionSpec as P

WIN = 96
NATOM = 64


GROUP = 8


def spread_kernel(ids_ref, values_ref, out_ref):
    per, points, wide = out_ref.shape
    slots = ids_ref.shape[1]
    columns = lax.broadcasted_iota(jnp.int32, (slots, wide), 1)
    for j in range(per):
        place = jnp.where(columns == ids_ref[0, :, j:j + 1], 1.0, 0.0).astype(jnp.bfloat16)
        out = jnp.dot(values_ref[j], place, preferred_element_type=jnp.float32)
        out_ref[j] = out.astype(jnp.bfloat16)


def spread(ids, values, wide):
    batches, points, slots = values.shape
    per = next(n for n in (4, 2, 1) if batches % n == 0 and n * wide <= 4096)
    ids = ids.reshape(batches // per, per, slots).transpose(0, 2, 1)
    return pl.pallas_call(
        spread_kernel,
        grid=(batches // per,),
        in_specs=[
            pl.BlockSpec((1, slots, per), lambda b: (b, 0, 0)),
            pl.BlockSpec((per, points, slots), lambda b: (b, 0, 0)),
        ],
        out_specs=pl.BlockSpec((per, points, wide), lambda b: (b, 0, 0)),
        out_shape=jax.ShapeDtypeStruct((batches, points, wide), jnp.bfloat16),
        compiler_params=pltpu.CompilerParams(dimension_semantics=("arbitrary",)),
        cost_estimate=pl.CostEstimate(
            flops=2 * batches * points * slots * wide,
            bytes_accessed=2 * batches * points * (slots + wide),
            transcendentals=0,
        ),
    )(ids, values)


def density_kernel(atom_ref, spread_ref, window_ref, occ_ref, harm_ref, out_ref, mom, rows):
    per = spread_ref.shape[0]
    _, points, wide = spread_ref.shape
    states = window_ref.shape[1]
    cols, _, share = out_ref.shape
    parts = harm_ref.shape[0]
    i = pl.program_id(0)
    first = pl.multiple_of(i * per, per)
    inner = lax.rem(first, GROUP)

    @pl.when(i == 0)
    def _():
        mom[...] = jnp.zeros_like(mom)

    step = min(256, states)
    lanes = min(128, step)
    pair = min(2, per)
    for j in range(0, per, pair):
        values = spread_ref[j:j + pair].reshape(pair * points, wide)
        total = jnp.zeros((pair * points, lanes), jnp.float32)
        for start in range(0, states, step):
            orbital = jnp.dot(
                values, window_ref[:, start:start + step], preferred_element_type=jnp.float32
            )
            scaled = orbital * orbital * occ_ref[:, start:start + step]
            for lane in range(0, step, lanes):
                total = total + scaled[:, lane:lane + lanes]
        for k in range(pair):
            piece = total[k * points:(k + 1) * points].T
            rows[pl.ds(inner + j + k, 1), :] = jnp.sum(piece, axis=0, keepdims=True)

    @pl.when(inner + per == GROUP)
    def _():
        base = pl.multiple_of(first + per - GROUP, GROUP)
        density = rows[...]
        for c in range(cols):
            out_ref[c, pl.ds(base, GROUP), :] = density[:, c * share:(c + 1) * share]
        local = jnp.sum(harm_ref[...] * density[None], axis=2, keepdims=True)
        spots = lax.broadcasted_iota(jnp.int32, (GROUP, NATOM), 0)
        atoms = jnp.zeros((GROUP, NATOM), jnp.int32)
        for k in range(GROUP):
            atoms = jnp.where(spots == k, atom_ref[base + k], atoms)
        lanes_of = lax.broadcasted_iota(jnp.int32, (GROUP, NATOM), 1)
        member = jnp.where(atoms == lanes_of, 1.0, 0.0)
        mom[...] += local * member[None]

    @pl.when(i == pl.num_programs(0) - 1)
    def _():
        done = jnp.sum(mom[...], axis=1)
        batches = pl.num_programs(0) * per
        for c in range(cols):
            out_ref[c, pl.ds(batches, parts), :NATOM] = done


def densities(batch_atom, spreads, window, occupation, harmonics, cols):
    batches, points, wide = spreads.shape
    states = window.shape[1]
    parts = harmonics.shape[1]
    share = points // cols
    per = GROUP if wide <= 1024 else 2
    height = batches + -(-parts // GROUP) * GROUP
    ratio = GROUP // per
    return pl.pallas_call(
        density_kernel,
        grid_spec=pltpu.PrefetchScalarGridSpec(
            num_scalar_prefetch=1,
            grid=(batches // per,),
            in_specs=[
                pl.BlockSpec((per, points, wide), lambda b, a: (b, 0, 0)),
                pl.BlockSpec((wide, states), lambda b, a: (0, 0)),
                pl.BlockSpec((1, states), lambda b, a: (0, 0)),
                pl.BlockSpec((parts, GROUP, points), lambda b, a: (0, b // ratio, 0)),
            ],
            out_specs=pl.BlockSpec((cols, height, share), lambda b, a: (0, 0, 0)),
            scratch_shapes=[
                pltpu.VMEM((parts, GROUP, NATOM), jnp.float32),
                pltpu.VMEM((GROUP, points), jnp.float32),
            ],
        ),
        out_shape=jax.ShapeDtypeStruct((cols, height, share), jnp.float32),
        compiler_params=pltpu.CompilerParams(dimension_semantics=("arbitrary",)),
        cost_estimate=pl.CostEstimate(
            flops=2 * batches * points * wide * states,
            bytes_accessed=2 * batches * points * wide,
            transcendentals=0,
        ),
    )(batch_atom, spreads, window, occupation[None, :], jnp.transpose(harmonics, (1, 0, 2)))


def shards(coeffs, occupation, basis_on_grid, basis_map, basis_count, batch_atom, harmonics):
    batches, points, slots = basis_on_grid.shape
    owned = coeffs.shape[0]
    owners = lax.axis_size("row")
    wide = owners * WIN
    if wide == owned:
        outgoing = coeffs
    else:
        target = lax.broadcasted_iota(jnp.int32, (owners, WIN), 0)
        offset = lax.broadcasted_iota(jnp.int32, (owners, WIN), 1)
        outgoing = jnp.take(coeffs, jnp.mod(target * WIN + offset, owned).reshape(-1), axis=0)
    window = lax.all_to_all(outgoing, "row", split_axis=0, concat_axis=0, tiled=True)
    start = jnp.mod(lax.axis_index("row") * WIN, owned)
    source = basis_map // owned
    within = jnp.mod(basis_map % owned - start, owned)
    local_ids = source * WIN + within
    slot_ids = lax.broadcasted_iota(jnp.int32, (batches, slots), 1)
    local_ids = jnp.where(slot_ids < basis_count[:, None], local_ids, -1)
    spreads = spread(local_ids, basis_on_grid, wide)
    cols = lax.axis_size("col")
    parts = harmonics.shape[1]
    packed = densities(batch_atom, spreads, window, occupation, harmonics, cols)
    summed = jnp.sum(lax.all_to_all(packed, "col", split_axis=0, concat_axis=0, tiled=True), axis=0)
    density = summed[:batches]
    mine = jnp.broadcast_to(summed[None, batches:], (owners,) + summed[batches:].shape)
    gathered = lax.all_to_all(mine, "row", split_axis=0, concat_axis=0, tiled=True)
    moments = jnp.sum(gathered, axis=0)[:parts, :NATOM].T
    return (density, moments)


def solution(mesh):
    placed = (
        P("row", "col"),
        P("col"),
        P("row", None, None),
        P("row", None),
        P("row"),
        P("row"),
        P("row", None, None),
    )
    return jax.shard_map(
        shards, mesh=mesh, in_specs=placed, out_specs=(P("row", "col"), P()), check_vma=False
    )
```

time: 163 us -> 102 us (0.63)
  blocking collectives: 41.8 us -> 13 us
  Pallas kernels: 88.8 us -> 66.2 us
  between operations: 14.1 us -> 0.66 us
  waiting for transfers between devices: 0.02 us -> 5.95 us
  local copies, waits for them, and re-layouts: 10.1 us -> 5.38 us
  starting transfers between devices: 5.25 us -> 9.02 us
    psum x1 -> x0, blocking collectives: 41.8 us -> none  [shards(): moments = lax.psum(atom_part, ('row', 'col')).T]
    pallas_call x1, Pallas kernels: 40.8 us -> 26.6 us  [spread(): pl.pallas_call(spread_kernel, grid=(batches // per,), in_specs=[pl.BlockS...]
    all_to_all x0 -> x1, blocking collectives: none -> 13 us  [shards(): lax.all_to_all(packed, 'col', split_axis=0, concat_axis=0, tiled=True)]
    pallas_call x1, Pallas kernels: 48.1 us -> 39.5 us  [densities(): pl.pallas_call(density_kernel, grid_spec=pltpu.PrefetchScalarGridSpec(num...]
    unnamed x6 -> x2, local copies, waits for them, and re-layouts: 8.24 us -> 1.18 us
    all_to_all x0 -> x1, waiting for transfers between devices: none -> 5.94 us  [shards(): lax.all_to_all(mine, 'row', split_axis=0, concat_axis=0, tiled=True)]
    all_to_all x0 -> x1, starting transfers between devices: none -> 3.81 us  [shards(): lax.all_to_all(mine, 'row', split_axis=0, concat_axis=0, tiled=True)]
    reshape x0 -> x2, local copies, waits for them, and re-layouts: none -> 2.29 us  [spread(): ids = ids.reshape(batches // per, per, slots).transpose(0, 2, 1)]
  transfers between devices with their start and end apart: 2 -> 2, of which waited for: 0 -> 1; matrix products, arithmetic and copies ran while one was open for 5% -> 4% of each run, Pallas kernels for 25% -> 26%
where the time goes in v2:
time: 102 us; the launch traced here: 101 us
  Pallas kernels  66.2 us (65%)
  blocking collectives  13 us (13%)
  starting transfers between devices  9.02 us (9%)
  waiting for transfers between devices  5.95 us (6%)
  local copies, waits for them, and re-layouts  5.38 us (5%)
  other arithmetic  1.06 us (1%)
    pallas_call x1, Pallas kernels, densities(): pl.pallas_call(density_kernel, grid_spec=pltpu.PrefetchScalarGridSpec(num...  39.5 us
    pallas_call x1, Pallas kernels, spread(): pl.pallas_call(spread_kernel, grid=(batches // per,), in_specs=[pl.BlockS...  26.6 us
    all_to_all x1, blocking collectives, shards(): lax.all_to_all(packed, 'col', split_axis=0, concat_axis=0, tiled=True)  13 us
    all_to_all x1, waiting for transfers between devices, shards(): lax.all_to_all(mine, 'row', split_axis=0, concat_axis=0, tiled=True)  5.94 us
    all_to_all x1, starting transfers between devices, shards(): lax.all_to_all(outgoing, 'row', split_axis=0, concat_axis=0, tiled=True)  5.21 us
    all_to_all x1, starting transfers between devices, shards(): lax.all_to_all(mine, 'row', split_axis=0, concat_axis=0, tiled=True)  3.81 us
    reshape x2, local copies, waits for them, and re-layouts, spread(): ids = ids.reshape(batches // per, per, slots).transpose(0, 2, 1)  2.29 us
  transfers between devices with their start and end apart: 2, of which 1 were waited for; matrix products, arithmetic and copies ran while one was open for 4% of the time, Pallas kernels for 26%

profile of v2, /device:TPU:0, one launch (start us, length us, event | category | flops | bytes accessed | tf_op | source)
XLA Modules:
  0.0 101.2 jit_solution(3701024904565456759)
XLA Ops:
  0.6 5.2 %all-to-all-start = ((bf16[8,96,1024]{2,1,0:T(8,128)(2,1)}), bf16[8,96,1024]{2,1,0:T(8,128)(2,1)S(1)}, u32[]{:S(2)}, u32[]{:S(2)}) async-start(bf16[8,96,1024]{2,1,0:T(8,128)(2,1)} %bitcast.8), calls=%async_computation | async-start | bytes 3145728 | tf_op jit(solution)/shard_map/all_to_all | solution.py:147
  5.8 1.0 %fusion.2 = s32[40,512]{1,0:T(8,128)S(1)} fusion(s32[40,512]{1,0:T(8,128)} %param.10, s32[]{:T(128)S(6)} %select_n.28, s32[40]{0:T(128)} %param.11), kind=kLoop, calls=%fused_computation.5 | loop fusion | flops 471040 | bytes 164004 | tf_op jit(solution)/shard_map/jit(_where)/select_n | solution.py:153
  6.9 2.3 %copy.10 = s32[10,4,512]{1,2,0:T(8,128)} copy(s32[10,4,512]{2,1,0:T(4,128)S(1)} %reshape.11) | data formatting | bytes 163840 | tf_op jit(solution)/shard_map/reshape | solution.py:28
  9.2 26.6 %shard_map.86.spread_ref = bf16[40,512,768]{2,1,0:T(8,128)(2,1)} custom-call(s32[10,512,4]{2,1,0:T(8,128)} %bitcast.7, bf16[40,512,512]{2,1,0:T(8,128)(2,1)} %values_ref.1), custom_call_target="tpu_custom_call" | custom-call | flops 16106127360 | bytes 52428800 | tf_op jit(solution)/shard_map/pallas_call | solution.py:29
  35.8 0.0 all-to-all-done
  35.8 0.0 copy-start
  35.8 1.2 %copy-done = bf16[8,96,1024]{2,1,0:T(8,128)(2,1)} copy-done((bf16[8,96,1024]{2,1,0:T(8,128)(2,1)}, bf16[8,96,1024]{2,1,0:T(8,128)(2,1)S(1)}, u32[]{:S(2)}) %copy-start) | copy-done | bytes 1572888
  37.0 39.5 %shard_map.87 = f32[4,96,128]{2,1,0:T(8,128)} custom-call(s32[40]{0:T(128)} %atom_ref.1, bf16[40,512,768]{2,1,0:T(8,128)(2,1)} %shard_map.86.spread_ref, bf16[768,1024]{1,0:T(8,128)(2,1)} %bitcast.9, f32[1,1024]{1,0:T(1,128)} %bitcast.11, f32[49,40,512]{2,1,0:T(8,128)} %bitcast.10), custom_call_target="tpu_custom_call" | custom-call | flops 32212254720 | bytes 31457280 | tf_op jit(solution)/shard_map/pallas_call | solution.py:109
  76.5 13.0 %all_to_all.21 = f32[4,96,128]{2,1,0:T(8,128)S(1)} all-to-all(f32[4,96,128]{2,1,0:T(8,128)} %shard_map.87), channel_id=1, replica_groups=mesh['row'=8,'col'=4] {'col'}, dimensions={0} | all-to-all | bytes 393216 | tf_op jit(solution)/shard_map/all_to_all | solution.py:158
  89.5 0.7 broadcast_in_dim.7
  90.2 3.8 %all-to-all-start.2 = ((f32[8,56,128]{2,1,0:T(8,128)}), f32[8,56,128]{2,1,0:T(8,128)S(1)}, u32[]{:S(2)}, u32[]{:S(2)}) async-start(f32[8,56,128]{2,1,0:T(8,128)} %broadcast_in_dim.7), calls=%async_computation.2 | async-start | bytes 458752 | tf_op jit(solution)/shard_map/all_to_all | solution.py:161
  94.0 0.6 slice.12
  94.6 5.9 %all-to-all-done.2 = f32[8,56,128]{2,1,0:T(8,128)S(1)} async-done(((f32[8,56,128]{2,1,0:T(8,128)}), f32[8,56,128]{2,1,0:T(8,128)S(1)}, u32[]{:S(2)}, u32[]{:S(2)}) %all-to-all-start.2) | async-done | bytes 229408 | tf_op jit(solution)/shard_map/all_to_all | solution.py:161
  100.6 0.6 slice_bitcast_fusion
  (4 shorter events, 0.1 us)
Async XLA Ops:
  0.6 35.2 %all-to-all-start = ((bf16[8,96,1024]{2,1,0:T(8,128)(2,1)}), bf16[8,96,1024]{2,1,0:T(8,128)(2,1)S(1)}, u32[]{:S(2)}, u32[]{:S(2)}) async-start(bf16[8,96,1024]{2,1,0:T(8,128)(2,1)} %bitcast.8), calls=%async_computation | async-start | bytes 3145728 | tf_op jit(solution)/shard_map/all_to_all | solution.py:147
  35.8 1.2 %copy-start = (bf16[8,96,1024]{2,1,0:T(8,128)(2,1)}, bf16[8,96,1024]{2,1,0:T(8,128)(2,1)S(1)}, u32[]{:S(2)}) copy-start(bf16[8,96,1024]{2,1,0:T(8,128)(2,1)S(1)} %all-to-all-done) | copy-start | bytes 4718596
  90.2 10.4 %all-to-all-start.2 = ((f32[8,56,128]{2,1,0:T(8,128)}), f32[8,56,128]{2,1,0:T(8,128)S(1)}, u32[]{:S(2)}, u32[]{:S(2)}) async-start(f32[8,56,128]{2,1,0:T(8,128)} %broadcast_in_dim.7), calls=%async_computation.2 | async-start | bytes 458752 | tf_op jit(solution)/shard_map/all_to_all | solution.py:161
